TPU v7x, 256 devices: a whole 4x4x8 slice. The times are simulated.
256 devices in a mesh: tok: 16 (over y, x), ch: 16 (over z, core).
Axes of the slice: x: 4, y: 4, z: 8, core: 2. Of those that a mesh axis runs over, the one named last changes fastest.
Arguments:
- tokens: bfloat16 [256, 16384], P('tok', 'ch'), may hold values from -64 to 64
- probe: int32 [256, 16384], P('tok', 'ch'), may hold values from 0 to 1
- signs: int32 [16384], P('ch'), may hold values from 0 to 1
- gate_weight: bfloat16 [16384, 26624], P('ch', 'tok'), may hold values from -0.046875 to 0.046875
- up_weight: bfloat16 [16384, 26624], P('ch', 'tok'), may hold values from -0.046875 to 0.046875
- down_weight: bfloat16 [26624, 16384], P('tok', 'ch'), may hold values from -0.0390625 to 0.0390625
Outputs:
- rotated_product: float32 [256, 16384], P('tok', 'ch')
- diagonal_estimate: float32 [16384], P('ch')
All inputs are finite; a program needn't handle non-finite values.
Results may differ from a plain program's by a relative error of at most 0.004.
Values may be sent and summed in bfloat16 or wider, within the bound.
No kernel may reach another device: no remote copies, remote signals or barrier semaphores. Data moves between devices by JAX's collectives and lax.ppermute only.
A program may use at most 128 MiB of HBM per device.

v0:
```python
import math
import jax
import jax.numpy as jnp
from jax import lax
from jax.sharding import PartitionSpec as P

D = 16384


def partner_2(value, axis, stride):
    mask = 2**stride
    pairs = [(source, source ^ mask) for source in range(lax.axis_size(axis))]
    return lax.ppermute(value, axis, pairs)


def sign_table(length):
    indices = jnp.arange(length, dtype=jnp.int32)
    parity = jnp.zeros((length, length), jnp.int32)
    for bit_pos in range(length.bit_length() - 1):
        parity = parity + (indices[:, None] >> bit_pos & 1) * (indices[None, :] >> bit_pos & 1)
    return jnp.where(parity % 2 == 0, 1.0, -1.0).astype(jnp.float32)


def cross_pairs(values):
    my_index = lax.axis_index("ch")
    for bit_pos in range(lax.axis_size("ch").bit_length() - 1):
        partner = partner_2(values, "ch", bit_pos)
        upper_half = my_index >> bit_pos & 1 == 1
        values = jnp.where(upper_half, partner - values, values + partner)
    return values


def cross_section(values):
    return cross_pairs(values)


def grad_product(gate_piece, up_piece, gate_weight, up_weight):
    contract = (((1,), (1,)), ((), ()))
    first_term = lax.dot_general(
        gate_piece, gate_weight, contract, preferred_element_type=jnp.float32
    )
    return first_term + lax.dot_general(
        up_piece, up_weight, contract, preferred_element_type=jnp.float32
    )


def on_device(tokens, probe, signs, gate_weight, up_weight, down_weight):
    tok_rows, channels = tokens.shape
    total_rows = tok_rows * lax.axis_size("tok")
    root_scale = 1.0 / math.sqrt(D)
    hadamard = sign_table(channels)
    probe_signs = (2 * probe - 1).astype(jnp.float32)
    channel_signs = (2 * signs - 1).astype(jnp.float32)
    start_local = jnp.dot(
        (probe_signs * channel_signs[None, :]).astype(jnp.bfloat16),
        hadamard.astype(jnp.bfloat16),
        preferred_element_type=jnp.float32,
    )
    tangent = (cross_section(start_local) * root_scale).astype(jnp.bfloat16)
    all_tokens, all_tangent = (
        lax.all_gather(tokens, "tok", axis=0, tiled=True),
        lax.all_gather(tangent, "tok", axis=0, tiled=True),
    )
    inputs = jnp.stack([all_tokens, all_tangent], axis=1)
    gate_part = jnp.einsum("rsd,df->rsf", inputs, gate_weight, preferred_element_type=jnp.float32)
    up_part = jnp.einsum("rsd,df->rsf", inputs, up_weight, preferred_element_type=jnp.float32)
    summed = lax.psum_scatter(
        jnp.stack([gate_part, up_part], axis=2), "ch", scatter_dimension=0, tiled=True
    )
    gate_pre = summed[:, 0, 0]
    up_pre = summed[:, 0, 1]
    gate_tan = summed[:, 1, 0]
    up_tan = summed[:, 1, 1]
    sigmoid_gate = jax.nn.sigmoid(gate_pre)
    activated = gate_pre * sigmoid_gate
    slope_term = sigmoid_gate * (1.0 + gate_pre * (1.0 - sigmoid_gate))
    hidden_tan = (slope_term * gate_tan * up_pre + activated * up_tan).astype(jnp.bfloat16)
    out_part = jnp.dot(
        lax.all_gather(hidden_tan, "ch", axis=0, tiled=True),
        down_weight,
        preferred_element_type=jnp.float32,
    )
    out_tangent = lax.psum(out_part, "tok").astype(jnp.bfloat16)
    piece = out_tangent
    back_hidden = lax.psum_scatter(
        lax.dot_general(
            piece, down_weight, (((1,), (1,)), ((), ())), preferred_element_type=jnp.float32
        ),
        "ch",
        scatter_dimension=0,
        tiled=True,
    )
    back_gate = (back_hidden * up_pre * slope_term).astype(jnp.bfloat16)
    back_up = (back_hidden * activated).astype(jnp.bfloat16)
    stacked = jnp.stack([back_gate, back_up], axis=1)
    piece = lax.all_gather(stacked, "ch", axis=0, tiled=True)
    in_part = grad_product(piece[:, 0], piece[:, 1], gate_weight, up_weight)
    back_tokens = lax.psum_scatter(in_part, "tok", scatter_dimension=0, tiled=True)
    local_back = jnp.dot(
        back_tokens, hadamard, precision=lax.Precision.HIGHEST, preferred_element_type=jnp.float32
    )
    rotated_product = cross_section(local_back) * root_scale * channel_signs[None, :]
    token_terms = jnp.sum(probe_signs * rotated_product, axis=0)
    diagonal_estimate = lax.psum(token_terms, "tok") / total_rows
    return (rotated_product, diagonal_estimate)


def solution(mesh):
    placed = (
        P("tok", "ch"),
        P("tok", "ch"),
        P("ch"),
        P("ch", "tok"),
        P("ch", "tok"),
        P("tok", "ch"),
    )
    return jax.shard_map(
        on_device, mesh=mesh, in_specs=placed, out_specs=(P("tok", "ch"), P("ch")), check_vma=False
    )
```

profile of v0, /device:TPU:32, one launch (start us, length us, event | category | flops | bytes accessed | tf_op | source)
XLA Modules:
  0.0 515.5 jit_solution(10228923519675699118)
XLA Ops:
  8.1 6.5 %fusion.3 = pred[1024,1024]{1,0:T(32,128)(4,1)S(1)} fusion(s32[1024]{0:T(1024)S(1)} %get-tuple-element.6, s32[1024]{0:T(1024)S(1)} %get-tuple-element.7, s32[1024]{0:T(1024)S(1)} %get-tuple-element.8, s32[1024]{0:T(1024)S(1)} %get-tuple-element.9, s32[1024]{0:T(1024)S(1)} %get-tuple-element.10, s32[1024]{0:T(1024)S(1)} %get-tuple-element.11, ...), kind=kLoop, calls=%fused_computation.8 | loop fusion | flops 32505856 | bytes 1089536 | tf_op jit(solution)/shard_map/eq | solution.py:21
  15.6 1.4 fusion.14
  17.0 1.4 collective-permute-done
  19.2 1.9 collective-permute-start.1
  21.2 2.5 collective-permute-done.1
  24.5 3.4 collective-permute-start.2
  27.9 2.3 collective-permute-done.2
  30.2 6.1 %collective-permute-start.3 = (f32[16,1024]{1,0:T(8,128)S(1)}, f32[16,1024]{1,0:T(8,128)S(1)}, u32[]{:S(2)}, u32[]{:S(2)}) collective-permute-start(f32[16,1024]{1,0:T(8,128)S(1)} %add_select_fusion.4), channel_id=1, source_target_pairs={{0,8},{1,9},{2,10},{3,11},{4,12},{5,13},{6,14},{7,15},{8,0},{9,1},... | collective-permute-start | bytes 196616 | tf_op jit(solution)/shard_map/ppermute | solution.py:13
  36.3 24.4 %all_gather.12 = bf16[256,1024]{1,0:T(8,128)(2,1)S(1)} all-gather(bf16[16,1024]{1,0:T(8,128)(2,1)} %param.6), channel_id=1, replica_groups=mesh['tok'=16,'ch'=16] {'tok'}, dimensions={0}, use_global_device_ids=true | all-gather | bytes 557056 | tf_op jit(solution)/shard_map/all_gather | solution.py:61
  60.7 23.3 %all_gather.13 = bf16[256,1024]{1,0:T(8,128)(2,1)S(1)} all-gather(bf16[16,1024]{1,0:T(8,128)(2,1)S(1)} %multiply_convert_fusion.2), channel_id=1, replica_groups=mesh['tok'=16,'ch'=16] {'tok'}, dimensions={0}, use_global_device_ids=true | all-gather | bytes 557056 | tf_op jit(solution)/shard_map/all_gather | solution.py:62
  84.0 4.0 fusion.11
  88.0 2.1 fusion.8
  90.1 3.3 pad_maximum_fusion
  93.4 60.3 %reduce-scatter.4.cloned.1.call-done = f32[16,2,2,1664]{3,0,1,2:T(8,128)} async-done(((f32[256,2,2,1664]{3,0,1,2:T(8,128)}), f32[16,2,2,1664]{3,0,1,2:T(8,128)}) %reduce-scatter.4.cloned.1.call-update) | async-done | bytes 426000 | tf_op jit(solution)/shard_map/reduce_scatter | solution.py:67
  153.7 1.1 fusion.24
  154.8 20.4 %all_gather.14 = bf16[256,1664]{1,0:T(8,128)(2,1)S(1)} all-gather(bf16[16,1664]{1,0:T(8,128)(2,1)S(1)} %fusion.24), channel_id=1, replica_groups=mesh['tok'=16,'ch'=16] {'ch'}, dimensions={0}, use_global_device_ids=true | all-gather | bytes 905216 | tf_op jit(solution)/shard_map/all_gather | solution.py:79
  175.3 4.1 fusion.41
  179.4 88.3 %all-reduce.1 = bf16[256,1024]{1,0:T(8,128)(2,1)} all-reduce(f32[256,1024]{1,0:T(8,128)} %fusion.41), channel_id=1, replica_groups=mesh['tok'=16,'ch'=16] {'tok'}, use_global_device_ids=true, to_apply=%region_1.2 | all-reduce | flops 262144 | bytes 1572864 | tf_op jit(solution)/shard_map/psum | solution.py:83
  267.7 4.5 fusion.42
  272.3 49.8 %reduce-scatter.6.cloned.1.call-done = f32[16,1664]{1,0:T(8,128)} async-done(((f32[256,1664]{1,0:T(8,128)}), f32[16,1664]{1,0:T(8,128)}) %reduce-scatter.6.cloned.1.call-update) | async-done | bytes 106512 | tf_op jit(solution)/shard_map/reduce_scatter | solution.py:85
  324.1 40.5 %all-gather.2.cloned.1.call-done = bf16[256,2,1664]{2,0,1:T(8,128)(2,1)} async-done(((bf16[16,2,1664]{2,0,1:T(8,128)(2,1)}), bf16[256,2,1664]{2,0,1:T(8,128)(2,1)}) %all-gather.2.cloned.1.call-update) | async-done | bytes 1703952 | tf_op jit(solution)/shard_map/all_gather | solution.py:96
  364.6 2.4 fusion.19
  367.3 2.1 convolution_add_fusion
  369.5 77.1 %reduce-scatter.8.cloned.1.call-done = f32[16,1024]{1,0:T(8,128)} async-done(((f32[256,1024]{1,0:T(8,128)}), f32[16,1024]{1,0:T(8,128)}) %reduce-scatter.8.cloned.1.call-update) | async-done | bytes 65552 | tf_op jit(solution)/shard_map/reduce_scatter | solution.py:98
  446.6 3.6 fusion
  450.2 1.2 collective-permute-done.4
  452.0 3.8 collective-permute-done.5
  455.8 2.6 collective-permute-start.6
  458.4 2.6 collective-permute-done.6
  461.1 5.0 collective-permute-start.7
  466.1 3.5 collective-permute-done.7
  470.3 38.1 %psum.15 = f32[1024]{0:T(1024)S(1)} all-reduce(f32[1024]{0:T(1024)S(1)} %get-tuple-element.2), channel_id=1, replica_groups=mesh['tok'=16,'ch'=16] {'tok'}, use_global_device_ids=true, to_apply=%region_5.6 | all-reduce | flops 1024 | bytes 8192 | tf_op jit(solution)/shard_map/psum | solution.py:104
  (42 shorter events, 7.8 us)
Async XLA Ops:
  7.2 80.8 %copy-start = (bf16[1024,1664]{1,0:T(8,128)(2,1)S(1)}, bf16[1024,1664]{1,0:T(8,128)(2,1)}, u32[]{:S(2)}) copy-start(bf16[1024,1664]{1,0:T(8,128)(2,1)} %param.9) | copy-start | bytes 10223620
  7.2 146.5 %reduce-scatter.4.cloned.1.call-start = ((), (), s32[]{:S(2)}) async-start(), calls=%async_computation.3 | async-start | bytes 7241728 | tf_op jit(solution)/shard_map/reduce_scatter | solution.py:67
  14.6 1.0 copy-start.1
  17.0 1.4 collective-permute-start
  19.2 4.5 collective-permute-start.1
  24.5 5.7 %collective-permute-start.2 = (f32[16,1024]{1,0:T(8,128)S(1)}, f32[16,1024]{1,0:T(8,128)S(1)}, u32[]{:S(2)}, u32[]{:S(2)}) collective-permute-start(f32[16,1024]{1,0:T(8,128)S(1)} %add_select_fusion.5), channel_id=1, source_target_pairs={{0,4},{1,5},{2,6},{3,7},{4,0},{5,1},{6,2},{7,3},{8,12},{9,13},{10,... | collective-permute-start | bytes 196616 | tf_op jit(solution)/shard_map/ppermute | solution.py:13
  30.2 30.4 %collective-permute-start.3 = (f32[16,1024]{1,0:T(8,128)S(1)}, f32[16,1024]{1,0:T(8,128)S(1)}, u32[]{:S(2)}, u32[]{:S(2)}) collective-permute-start(f32[16,1024]{1,0:T(8,128)S(1)} %add_select_fusion.4), channel_id=1, source_target_pairs={{0,8},{1,9},{2,10},{3,11},{4,12},{5,13},{6,14},{7,15},{8,0},{9,1},... | collective-permute-start | bytes 196616 | tf_op jit(solution)/shard_map/ppermute | solution.py:13
  93.4 228.7 %reduce-scatter.6.cloned.1.call-start = ((), (), s32[]{:S(2)}) async-start(), calls=%async_computation.4 | async-start | bytes 1810432 | tf_op jit(solution)/shard_map/reduce_scatter | solution.py:85
  272.2 92.4 %all-gather.2.cloned.1.call-start = ((), (), s32[]{:S(2)}) async-start(), calls=%async_computation.5 | async-start | bytes 1810432 | tf_op jit(solution)/shard_map/all_gather | solution.py:96
  323.8 122.8 %reduce-scatter.8.cloned.1.call-start = ((), (), s32[]{:S(2)}) async-start(), calls=%async_computation.6 | async-start | bytes 1114112 | tf_op jit(solution)/shard_map/reduce_scatter | solution.py:98
  364.6 2.5 copy-start.4
  364.6 2.7 copy-start.5
  367.3 98.8 %copy-start.3 = (s32[1024]{0:T(1024)S(1)}, s32[1024]{0:T(1024)}, u32[]{:S(2)}) copy-start(s32[1024]{0:T(1024)} %param.8) | copy-start | bytes 12292
  367.3 102.3 %copy-start.2 = (s32[16,1024]{1,0:T(8,128)S(1)}, s32[16,1024]{1,0:T(8,128)}, u32[]{:S(2)}) copy-start(s32[16,1024]{1,0:T(8,128)} %param.7) | copy-start | bytes 196612
  450.2 1.3 collective-permute-start.4
  451.4 4.4 collective-permute-start.5
  455.8 5.3 %collective-permute-start.6 = (f32[16,1024]{1,0:T(8,128)S(1)}, f32[16,1024]{1,0:T(8,128)S(1)}, u32[]{:S(2)}, u32[]{:S(2)}) collective-permute-start(f32[16,1024]{1,0:T(8,128)S(1)} %add_select_fusion.2), channel_id=1, source_target_pairs={{0,4},{1,5},{2,6},{3,7},{4,0},{5,1},{6,2},{7,3},{8,12},{9,13},{10,... | collective-permute-start | bytes 196616 | tf_op jit(solution)/shard_map/ppermute | solution.py:13
  461.1 8.5 %collective-permute-start.7 = (f32[16,1024]{1,0:T(8,128)S(1)}, f32[16,1024]{1,0:T(8,128)S(1)}, u32[]{:S(2)}, u32[]{:S(2)}) collective-permute-start(f32[16,1024]{1,0:T(8,128)S(1)} %add_select_fusion.1), channel_id=1, source_target_pairs={{0,8},{1,9},{2,10},{3,11},{4,12},{5,13},{6,14},{7,15},{8,0},{9,1},... | collective-permute-start | bytes 196616 | tf_op jit(solution)/shard_map/ppermute | solution.py:13
Sparse Core Ops, SparseCore 0:
  93.5 60.1 reduce-scatter.3
  272.3 49.7 reduce-scatter.5
  324.1 40.4 all-gather.1
  369.6 76.9 reduce-scatter.7
where the time goes:
time: 516 us
  waiting for transfers between devices  245 us (47%)
  blocking collectives  195 us (38%)
  matrix products  24.3 us (5%)
  starting transfers between devices  19.8 us (4%)
  other arithmetic  16.4 us (3%)
  between operations  13.9 us (3%)
    psum x1, blocking collectives, on_device(): out_tangent = lax.psum(out_part, 'tok').astype(jnp.bfloat16)  88.3 us
    reduce_scatter x1, waiting for transfers between devices, on_device(): lax.psum_scatter(in_part, 'tok', scatter_dimension=0, tiled=True)  77.1 us
    reduce_scatter x1, waiting for transfers between devices, on_device(): lax.psum_scatter(jnp.stack([gate_part, up_part], axis=2), 'ch', scatter_d...  60.3 us
    reduce_scatter x1, waiting for transfers between devices, on_device(): lax.psum_scatter(lax.dot_general(piece, down_weight, (((1,), (1,)), ((),...  49.8 us
    all_gather x1, waiting for transfers between devices, on_device(): piece = lax.all_gather(stacked, 'ch', axis=0, tiled=True)  40.5 us
    psum x1, blocking collectives, on_device(): diagonal_estimate = lax.psum(token_terms, 'tok') / total_rows  38.1 us
    all_gather x1, blocking collectives, on_device(): lax.all_gather(tokens, 'tok', axis=0, tiled=True)  24.4 us
    all_gather x1, blocking collectives, on_device(): lax.all_gather(tangent, 'tok', axis=0, tiled=True)  23.3 us
  transfers between devices with their start and end apart: 12, of which 11 were waited for; matrix products, arithmetic and copies ran while one was open for 0% of the time, Pallas kernels for 0%

commit v1 on v0

--- a/solution.py
+++ b/solution.py
@@ -80,7 +80,7 @@
         down_weight,
         preferred_element_type=jnp.float32,
     )
-    out_tangent = lax.psum(out_part, "tok").astype(jnp.bfloat16)
+    out_tangent = jnp.sum(lax.all_gather(out_part, "tok"), axis=0).astype(jnp.bfloat16)
     piece = out_tangent
     back_hidden = lax.psum_scatter(
         lax.dot_general(

time: 516 us -> 557 us (1.079)
  waiting for transfers between devices: 245 us -> 366 us
  blocking collectives: 195 us -> 106 us
  other arithmetic: 16.4 us -> 25.1 us
    all_gather x0 -> x1, waiting for transfers between devices: none -> 115 us  [on_device(): lax.all_gather(out_part, 'tok')]
    psum x1 -> x0, blocking collectives: 88.3 us -> none  [on_device(): out_tangent = lax.psum(out_part, 'tok').astype(jnp.bfloat16)]
    reduce_sum x0 -> x1, other arithmetic: none -> 8.62 us  [on_device(): jnp.sum(lax.all_gather(out_part, 'tok'), axis=0).astype(jnp.bfloat16)]
  transfers between devices with their start and end apart: 12 -> 13, of which waited for: 11 -> 12; matrix products, arithmetic and copies ran while one was open for 0% -> 0% of each run, Pallas kernels for 0% -> 0%
where the time goes in v1:
time: 557 us; the launch traced here: 556 us
  waiting for transfers between devices  366 us (66%)
  blocking collectives  106 us (19%)
  other arithmetic  25.1 us (5%)
  matrix products  24.3 us (4%)
  starting transfers between devices  19.9 us (4%)
  between operations  13.9 us (2%)
    all_gather x1, waiting for transfers between devices, on_device(): lax.all_gather(out_part, 'tok')  115 us
    reduce_scatter x1, waiting for transfers between devices, on_device(): lax.psum_scatter(in_part, 'tok', scatter_dimension=0, tiled=True)  77.1 us
    reduce_scatter x1, waiting for transfers between devices, on_device(): lax.psum_scatter(jnp.stack([gate_part, up_part], axis=2), 'ch', scatter_d...  60.2 us
    reduce_scatter x1, waiting for transfers between devices, on_device(): lax.psum_scatter(lax.dot_general(piece, down_weight, (((1,), (1,)), ((),...  55 us
    all_gather x1, waiting for transfers between devices, on_device(): piece = lax.all_gather(stacked, 'ch', axis=0, tiled=True)  40.7 us
    psum x1, blocking collectives, on_device(): diagonal_estimate = lax.psum(token_terms, 'tok') / total_rows  38.1 us
    all_gather x1, blocking collectives, on_device(): lax.all_gather(tokens, 'tok', axis=0, tiled=True)  24.4 us
    all_gather x1, blocking collectives, on_device(): lax.all_gather(tangent, 'tok', axis=0, tiled=True)  23.3 us
  transfers between devices with their start and end apart: 13, of which 12 were waited for; matrix products, arithmetic and copies ran while one was open for 0% of the time, Pallas kernels for 0%

profile of v1, /device:TPU:32, one launch (start us, length us, event | category | flops | bytes accessed | tf_op | source)
XLA Modules:
  0.0 556.4 jit_solution(2880315919128648910)
XLA Ops:
  8.1 6.5 %fusion.3 = pred[1024,1024]{1,0:T(32,128)(4,1)S(1)} fusion(s32[1024]{0:T(1024)S(1)} %get-tuple-element.6, s32[1024]{0:T(1024)S(1)} %get-tuple-element.7, s32[1024]{0:T(1024)S(1)} %get-tuple-element.8, s32[1024]{0:T(1024)S(1)} %get-tuple-element.9, s32[1024]{0:T(1024)S(1)} %get-tuple-element.10, s32[1024]{0:T(1024)S(1)} %get-tuple-element.11, ...), kind=kLoop, calls=%fused_computation.8 | loop fusion | flops 32505856 | bytes 1089536 | tf_op jit(solution)/shard_map/eq | solution.py:21
  15.6 1.4 fusion.14
  17.0 1.4 collective-permute-done
  19.2 1.9 collective-permute-start.1
  21.2 2.5 collective-permute-done.1
  24.6 3.4 collective-permute-start.2
  27.9 2.3 collective-permute-done.2
  30.2 6.1 %collective-permute-start.3 = (f32[16,1024]{1,0:T(8,128)S(1)}, f32[16,1024]{1,0:T(8,128)S(1)}, u32[]{:S(2)}, u32[]{:S(2)}) collective-permute-start(f32[16,1024]{1,0:T(8,128)S(1)} %add_select_fusion.4), channel_id=1, source_target_pairs={{0,8},{1,9},{2,10},{3,11},{4,12},{5,13},{6,14},{7,15},{8,0},{9,1},... | collective-permute-start | bytes 196616 | tf_op jit(solution)/shard_map/ppermute | solution.py:13
  36.3 24.4 %all_gather.18 = bf16[256,1024]{1,0:T(8,128)(2,1)S(1)} all-gather(bf16[16,1024]{1,0:T(8,128)(2,1)} %param.6), channel_id=1, replica_groups=mesh['tok'=16,'ch'=16] {'tok'}, dimensions={0}, use_global_device_ids=true | all-gather | bytes 557056 | tf_op jit(solution)/shard_map/all_gather | solution.py:61
  60.7 23.3 %all_gather.19 = bf16[256,1024]{1,0:T(8,128)(2,1)S(1)} all-gather(bf16[16,1024]{1,0:T(8,128)(2,1)S(1)} %multiply_convert_fusion.2), channel_id=1, replica_groups=mesh['tok'=16,'ch'=16] {'tok'}, dimensions={0}, use_global_device_ids=true | all-gather | bytes 557056 | tf_op jit(solution)/shard_map/all_gather | solution.py:62
  84.0 4.0 fusion.11
  88.0 2.1 fusion.8
  90.1 3.3 pad_maximum_fusion
  93.4 60.2 %reduce-scatter.4.cloned.1.call-done = f32[16,2,2,1664]{3,0,1,2:T(8,128)} async-done(((f32[256,2,2,1664]{3,0,1,2:T(8,128)}), f32[16,2,2,1664]{3,0,1,2:T(8,128)}) %reduce-scatter.4.cloned.1.call-update) | async-done | bytes 426000 | tf_op jit(solution)/shard_map/reduce_scatter | solution.py:67
  154.8 20.4 %all_gather.20 = bf16[256,1664]{1,0:T(8,128)(2,1)S(1)} all-gather(bf16[16,1664]{1,0:T(8,128)(2,1)S(1)} %fusion.24), channel_id=1, replica_groups=mesh['tok'=16,'ch'=16] {'ch'}, dimensions={0}, use_global_device_ids=true | all-gather | bytes 905216 | tf_op jit(solution)/shard_map/all_gather | solution.py:79
  175.2 4.1 fusion.41
  179.6 115.1 %all-gather.6.cloned.1.call-done = f32[4096,1024]{1,0:T(8,128)} async-done(((f32[256,1024]{1,0:T(8,128)}), f32[4096,1024]{1,0:T(8,128)}) %all-gather.6.cloned.1.call-update) | async-done | bytes 16777232 | tf_op jit(solution)/shard_map/all_gather | solution.py:83
  294.8 8.6 %reduce_sum.18 = bf16[256,1024]{1,0:T(8,128)(2,1)} reduce(f32[16,256,1024]{2,1,0:T(8,128)} %bitcast.78, f32[]{:T(128)} %constant.32.clone.1), dimensions={0}, to_apply=%region_1.2 | reduce | flops 3932160 | bytes 17301508 | tf_op jit(solution)/shard_map/reduce_sum | solution.py:83
  303.4 4.5 fusion.42
  308.0 55.0 %reduce-scatter.6.cloned.1.call-done = f32[16,1664]{1,0:T(8,128)} async-done(((f32[256,1664]{1,0:T(8,128)}), f32[16,1664]{1,0:T(8,128)}) %reduce-scatter.6.cloned.1.call-update) | async-done | bytes 106512 | tf_op jit(solution)/shard_map/reduce_scatter | solution.py:85
  364.8 40.7 %all-gather.4.cloned.1.call-done = bf16[256,2,1664]{2,0,1:T(8,128)(2,1)} async-done(((bf16[16,2,1664]{2,0,1:T(8,128)(2,1)}), bf16[256,2,1664]{2,0,1:T(8,128)(2,1)}) %all-gather.4.cloned.1.call-update) | async-done | bytes 1703952 | tf_op jit(solution)/shard_map/all_gather | solution.py:96
  405.5 2.4 fusion.19
  408.2 2.1 convolution_add_fusion
  410.4 77.1 %reduce-scatter.8.cloned.1.call-done = f32[16,1024]{1,0:T(8,128)} async-done(((f32[256,1024]{1,0:T(8,128)}), f32[16,1024]{1,0:T(8,128)}) %reduce-scatter.8.cloned.1.call-update) | async-done | bytes 65552 | tf_op jit(solution)/shard_map/reduce_scatter | solution.py:98
  487.5 3.6 fusion
  491.0 1.2 collective-permute-done.4
  492.9 3.8 collective-permute-done.5
  496.7 2.6 collective-permute-start.6
  499.3 2.6 collective-permute-done.6
  501.9 5.0 collective-permute-start.7
  507.0 3.5 collective-permute-done.7
  511.1 38.1 %psum.7 = f32[1024]{0:T(1024)S(1)} all-reduce(f32[1024]{0:T(1024)S(1)} %get-tuple-element.2), channel_id=1, replica_groups=mesh['tok'=16,'ch'=16] {'tok'}, use_global_device_ids=true, to_apply=%region_5.6 | all-reduce | flops 1024 | bytes 8192 | tf_op jit(solution)/shard_map/psum | solution.py:104
  (45 shorter events, 9.0 us)
Async XLA Ops:
  7.2 80.9 %copy-start = (bf16[1024,1664]{1,0:T(8,128)(2,1)S(1)}, bf16[1024,1664]{1,0:T(8,128)(2,1)}, u32[]{:S(2)}) copy-start(bf16[1024,1664]{1,0:T(8,128)(2,1)} %param.9) | copy-start | bytes 10223620
  7.2 146.5 %reduce-scatter.4.cloned.1.call-start = ((), (), s32[]{:S(2)}) async-start(), calls=%async_computation.3 | async-start | bytes 7241728 | tf_op jit(solution)/shard_map/reduce_scatter | solution.py:67
  14.6 1.0 copy-start.1
  17.0 1.4 collective-permute-start
  19.2 4.5 collective-permute-start.1
  24.6 5.7 %collective-permute-start.2 = (f32[16,1024]{1,0:T(8,128)S(1)}, f32[16,1024]{1,0:T(8,128)S(1)}, u32[]{:S(2)}, u32[]{:S(2)}) collective-permute-start(f32[16,1024]{1,0:T(8,128)S(1)} %add_select_fusion.5), channel_id=1, source_target_pairs={{0,4},{1,5},{2,6},{3,7},{4,0},{5,1},{6,2},{7,3},{8,12},{9,13},{10,... | collective-permute-start | bytes 196616 | tf_op jit(solution)/shard_map/ppermute | solution.py:13
  30.2 30.4 %collective-permute-start.3 = (f32[16,1024]{1,0:T(8,128)S(1)}, f32[16,1024]{1,0:T(8,128)S(1)}, u32[]{:S(2)}, u32[]{:S(2)}) collective-permute-start(f32[16,1024]{1,0:T(8,128)S(1)} %add_select_fusion.4), channel_id=1, source_target_pairs={{0,8},{1,9},{2,10},{3,11},{4,12},{5,13},{6,14},{7,15},{8,0},{9,1},... | collective-permute-start | bytes 196616 | tf_op jit(solution)/shard_map/ppermute | solution.py:13
  93.4 201.4 %all-gather.6.cloned.1.call-start = ((), (), s32[]{:S(2)}) async-start(), calls=%async_computation.7 | async-start | bytes 17825792 | tf_op jit(solution)/shard_map/all_gather | solution.py:83
  179.4 183.6 %reduce-scatter.6.cloned.1.call-start = ((), (), s32[]{:S(2)}) async-start(), calls=%async_computation.4 | async-start | bytes 1810432 | tf_op jit(solution)/shard_map/reduce_scatter | solution.py:85
  307.9 97.6 %all-gather.4.cloned.1.call-start = ((), (), s32[]{:S(2)}) async-start(), calls=%async_computation.5 | async-start | bytes 1810432 | tf_op jit(solution)/shard_map/all_gather | solution.py:96
  364.7 122.7 %reduce-scatter.8.cloned.1.call-start = ((), (), s32[]{:S(2)}) async-start(), calls=%async_computation.6 | async-start | bytes 1114112 | tf_op jit(solution)/shard_map/reduce_scatter | solution.py:98
  405.5 2.5 copy-start.4
  405.5 2.7 copy-start.5
  408.2 98.7 %copy-start.3 = (s32[1024]{0:T(1024)S(1)}, s32[1024]{0:T(1024)}, u32[]{:S(2)}) copy-start(s32[1024]{0:T(1024)} %param.8) | copy-start | bytes 12292
  408.2 102.2 %copy-start.2 = (s32[16,1024]{1,0:T(8,128)S(1)}, s32[16,1024]{1,0:T(8,128)}, u32[]{:S(2)}) copy-start(s32[16,1024]{1,0:T(8,128)} %param.7) | copy-start | bytes 196612
  491.0 1.3 collective-permute-start.4
  492.3 4.4 collective-permute-start.5
  496.7 5.3 collective-permute-start.6
  501.9 8.5 %collective-permute-start.7 = (f32[16,1024]{1,0:T(8,128)S(1)}, f32[16,1024]{1,0:T(8,128)S(1)}, u32[]{:S(2)}, u32[]{:S(2)}) collective-permute-start(f32[16,1024]{1,0:T(8,128)S(1)} %add_select_fusion.1), channel_id=1, source_target_pairs={{0,8},{1,9},{2,10},{3,11},{4,12},{5,13},{6,14},{7,15},{8,0},{9,1},... | collective-permute-start | bytes 196616 | tf_op jit(solution)/shard_map/ppermute | solution.py:13
Sparse Core Ops, SparseCore 0:
  93.5 60.1 reduce-scatter.3
  179.5 115.2 all-gather.5
  308.0 54.9 reduce-scatter.5
  364.9 40.5 all-gather.3
  410.5 76.9 reduce-scatter.7
